TPU v7x, 32 devices: a whole 2x2x4 slice. The times are simulated.
32 devices in a mesh: groups: 2 (over x), row: 8 (over z, y), col: 2 (over core).
Axes of the slice: x: 2, y: 2, z: 4, core: 2. Of those that a mesh axis runs over, the one named last changes fastest.
Arguments:
- pair_rep: bfloat16 [160, 80, 128], P(('groups', 'row'), 'col'), parts along dimension 0, as said below
- proj_weight: bfloat16 [128, 512], replicated, may hold values from -0.5 to 0.5
- gate_weight: bfloat16 [128, 128], replicated, may hold values from -0.5 to 0.5
- out_weight: bfloat16 [128, 128], replicated, may hold values from -0.5 to 0.5
Outputs:
- update: bfloat16 [160, 80, 128], P(('groups', 'row'), 'col'), parts along dimension 0
There are 2 independent parts, one for each index of `groups`. A program takes and returns all parts, laid end to end along the dimension named above; an argument that names none is the same for every part. Nothing has to cross between parts.
Inputs may be any that keep to these rules, and one draw needn't show every extreme that they name: `pair_rep`: real-valued pair features; each pair position and each channel carries its own scale factor between 1 and 10.
All inputs are finite; a program needn't handle non-finite values.
Results may differ from a plain program's by a relative error of at most 0.0078.
Values may be sent and summed in bfloat16 or wider, within the bound.
A program may use at most 128 MiB of HBM per device.

v0:
```python
import jax
import jax.numpy as jnp
from jax import lax
from jax.sharding import PartitionSpec as P


def layer_norm(values):
    average = jnp.mean(values, axis=-1, keepdims=True)
    centered = values - average
    spread = jnp.mean(centered * centered, axis=-1, keepdims=True)
    return centered * lax.rsqrt(spread + 1e-05)


def per_device(pair_rep, proj_weight, gate_weight, out_weight):
    rows_here, cols_here, channels = pair_rep.shape
    hidden = out_weight.shape[0]
    normed = layer_norm(pair_rep.astype(jnp.float32)).astype(jnp.bfloat16)
    flat_rows = normed.reshape(-1, channels)
    projected = jnp.dot(flat_rows, proj_weight, preferred_element_type=jnp.float32)
    left_side = (jax.nn.sigmoid(projected[:, :hidden]) * projected[:, hidden : 2 * hidden]).astype(
        jnp.bfloat16
    )
    right_side = (
        jax.nn.sigmoid(projected[:, 2 * hidden : 3 * hidden]) * projected[:, 3 * hidden :]
    ).astype(jnp.bfloat16)
    left_side = left_side.reshape(rows_here, cols_here, hidden)
    right_side = right_side.reshape(rows_here, cols_here, hidden)
    gating = jax.nn.sigmoid(jnp.dot(flat_rows, gate_weight, preferred_element_type=jnp.float32))
    left_full, right_strip = (
        lax.all_gather(left_side, "col", axis=1, tiled=True),
        lax.all_gather(right_side, "col", axis=1, tiled=True),
    )
    right_all = lax.all_gather(right_strip, "row", axis=0, tiled=True)
    right_mine = lax.dynamic_slice_in_dim(
        right_all, lax.axis_index("col") * cols_here, cols_here, 0
    )
    combined = jnp.einsum("ikc,jkc->ijc", left_full, right_mine, preferred_element_type=jnp.float32)
    tri_normed = layer_norm(combined).astype(jnp.bfloat16).reshape(-1, hidden)
    update = jnp.dot(tri_normed, out_weight, preferred_element_type=jnp.float32) * gating
    return update.astype(jnp.bfloat16).reshape(rows_here, cols_here, channels)


def solution(mesh):
    placed = (P(("groups", "row"), "col", None), P(), P(), P())
    return jax.shard_map(
        per_device,
        mesh=mesh,
        in_specs=placed,
        out_specs=P(("groups", "row"), "col", None),
        check_vma=False,
    )
```

profile of v0, /device:TPU:0, one launch (start us, length us, event | category | flops | bytes accessed | tf_op | source)
XLA Modules:
  0.0 72.3 jit_solution(2186208317133575420)
XLA Ops:
  6.5 0.0 copy-start
  6.5 0.0 all-gather.2.cloned.1.call-start
  6.5 1.1 %convert_reduce_fusion = f32[10,40]{1,0:T(8,128)S(1)} fusion(bf16[10,40,128]{2,1,0:T(8,128)(2,1)} %param.4), kind=kLoop, calls=%fused_computation.10 | loop fusion | flops 102000 | bytes 104000 | tf_op jit(solution)/shard_map/reduce_sum | solution.py:8
  7.6 1.1 %fusion.6 = f32[10,40]{1,0:T(8,128)S(1)} fusion(bf16[10,40,128]{2,1,0:T(8,128)(2,1)} %param.4, f32[10,40]{1,0:T(8,128)S(1)} %broadcast_multiply_fusion.1), kind=kLoop, calls=%fused_computation.13 | loop fusion | flops 204400 | bytes 105600 | tf_op jit(solution)/shard_map/reduce_sum | solution.py:10
  8.8 1.1 %fusion.7 = bf16[10,40,128]{2,1,0:T(8,128)(2,1)S(1)} fusion(bf16[10,40,128]{2,1,0:T(8,128)(2,1)} %param.4, f32[10,40]{1,0:T(8,128)S(1)} %add_rsqrt_fusion.1, f32[10,40]{1,0:T(8,128)S(1)} %broadcast_multiply_fusion.1), kind=kLoop, calls=%fused_computation.14 | loop fusion | flops 204800 | bytes 208000 | tf_op jit(solution)/shard_map/convert_element_type | solution.py:17
  9.8 0.0 copy-done
  9.8 0.3 fusion.17
  10.1 0.0 copy-start.2
  10.1 0.1 fusion.8
  10.2 2.2 %all_gather.9 = bf16[10,80,128]{2,1,0:T(8,128)(2,1)} all-gather(bf16[10,40,128]{2,1,0:T(8,128)(2,1)S(1)} %bitcast.19), channel_id=1, replica_groups=mesh['groups'=2,'row'=8,'col'=2] {'col'}, dimensions={1}, use_global_device_ids=true | all-gather | bytes 307200 | tf_op jit(solution)/shard_map/all_gather | solution.py:31
  12.4 0.0 all-gather.2.cloned.1.call-update
  12.5 2.0 %all_gather.11 = bf16[10,80,128]{2,1,0:T(8,128)(2,1)S(1)} all-gather(bf16[10,40,128]{2,1,0:T(8,128)(2,1)S(1)} %bitcast.18), channel_id=1, replica_groups=mesh['groups'=2,'row'=8,'col'=2] {'col'}, dimensions={1}, use_global_device_ids=true | all-gather | bytes 307200 | tf_op jit(solution)/shard_map/all_gather | solution.py:30
  14.4 0.4 copy.11
  14.9 0.0 copy-done.2
  14.9 0.2 fusion.2
  15.1 44.9 %all-gather.2.cloned.1.call-done = bf16[80,80,128]{2,1,0:T(8,128)(2,1)} async-done(((bf16[10,80,128]{2,1,0:T(8,128)(2,1)}), bf16[80,80,128]{2,1,0:T(8,128)(2,1)}) %all-gather.2.cloned.1.call-update) | async-done | bytes 1638416 | tf_op jit(solution)/shard_map/all_gather | solution.py:33
  60.0 1.2 %constant_dynamic-slice_fusion = bf16[40,80,128]{2,1,0:T(8,128)(2,1)S(1)} fusion(bf16[80,80,128]{2,1,0:T(8,128)(2,1)} %all-gather.2.cloned.1.call-done, s32[]{:T(128)S(6)} %select_n.3), kind=kLoop, calls=%fused_computation.31 | loop fusion | bytes 1638404 | tf_op jit(solution)/shard_map/dynamic_slice | solution.py:34
  61.2 1.6 %copy.13 = bf16[40,80,128]{1,0,2:T(8,128)(2,1)S(1)} copy(bf16[40,80,128]{2,1,0:T(8,128)(2,1)S(1)} %constant_dynamic-slice_fusion) | data formatting | bytes 1638400
  62.8 0.8 %fusion.16 = (f32[10,40]{1,0:T(8,128)S(1)}, f32[10,40,128]{1,0,2:T(8,128)S(1)}) fusion(bf16[40,80,128]{1,0,2:T(8,128)(2,1)S(1)} %copy.13, bf16[10,80,128]{1,0,2:T(8,128)(2,1)S(1)} %copy.11), kind=kOutput, calls=%fused_computation.32 | convolution fusion | flops 8242800 | bytes 1230400 | tf_op jit(solution)/shard_map/ikc,jkc->ijc/dot_general | solution.py:37
  63.6 0.2 multiply_reduce_fusion
  63.8 0.0 copy-start.1
  63.9 0.1 multiply_convert_fusion
  64.0 0.4 copy.12
  64.4 0.3 copy-done.1
  64.6 0.8 %fusion.3 = bf16[400,128]{1,0:T(8,128)(2,1)} fusion(f32[400,128]{1,0:T(8,128)S(1)} %fusion.2, bf16[400,128]{1,0:T(8,128)(2,1)S(1)} %bitcast.15, bf16[128,128]{1,0:T(8,128)(2,1)S(1)} %copy-done.1), kind=kOutput, calls=%fused_computation.6 | convolution fusion | flops 13209600 | bytes 442368 | tf_op jit(solution)/shard_map/dot_general | solution.py:39
  (4 shorter events, 0.0 us)
Async XLA Ops:
  6.5 3.3 %copy-start = (bf16[128,512]{1,0:T(8,128)(2,1)S(1)}, bf16[128,512]{1,0:T(8,128)(2,1)}, u32[]{:S(2)}) copy-start(bf16[128,512]{1,0:T(8,128)(2,1)} %param.5) | copy-start | bytes 393220
  6.5 53.5 %all-gather.2.cloned.1.call-start = ((), (), s32[]{:S(2)}) async-start(), calls=%async_computation | async-start | bytes 1843200 | tf_op jit(solution)/shard_map/all_gather | solution.py:33
  10.1 4.8 %copy-start.2 = (bf16[128,128]{1,0:T(8,128)(2,1)S(1)}, bf16[128,128]{1,0:T(8,128)(2,1)}, u32[]{:S(2)}) copy-start(bf16[128,128]{1,0:T(8,128)(2,1)} %param.6) | copy-start | bytes 98308
  63.8 0.8 %copy-start.1 = (bf16[128,128]{1,0:T(8,128)(2,1)S(1)}, bf16[128,128]{1,0:T(8,128)(2,1)}, u32[]{:S(2)}) copy-start(bf16[128,128]{1,0:T(8,128)(2,1)} %param.7) | copy-start | bytes 98308
Sparse Core Ops, SparseCore 0:
  12.6 47.3 all-gather.1
where the time goes:
time: 72.6 us; the launch traced here: 72.3 us
  waiting for transfers between devices  45 us (62%)
  between operations  13.5 us (19%)
  blocking collectives  4.17 us (6%)
  local copies, waits for them, and re-layouts  3.85 us (5%)
  other arithmetic  3.7 us (5%)
  matrix products  2.09 us (3%)
    all_gather x1, waiting for transfers between devices, per_device(): right_all = lax.all_gather(right_strip, 'row', axis=0, tiled=True)  44.9 us
    all_gather x1, blocking collectives, per_device(): lax.all_gather(right_side, 'col', axis=1, tiled=True)  2.22 us
    all_gather x1, blocking collectives, per_device(): lax.all_gather(left_side, 'col', axis=1, tiled=True)  1.95 us
    unnamed x7, local copies, waits for them, and re-layouts  1.87 us
  transfers between devices with their start and end apart: 1, of which 1 were waited for; matrix products, arithmetic and copies ran while one was open for 1% of the time, Pallas kernels for 0%

commit v1 on v0

v1 whole, which is shorter than its diff:
```python
import functools

import jax
import jax.numpy as jnp
from jax import lax
from jax.experimental import pallas as pl
from jax.experimental.pallas import tpu as pltpu
from jax.sharding import PartitionSpec as P

MESH = pl.DeviceIdType.MESH
F32 = jnp.float32
BF16 = jnp.bfloat16


def layer_norm(values):
    average = jnp.mean(values, axis=-1, keepdims=True)
    centered = values - average
    spread = jnp.mean(centered * centered, axis=-1, keepdims=True)
    return centered * lax.rsqrt(spread + 1e-05)


def kernel(
    n, rows, cols, chunks, x_ref, wp_ref, wg_ref, wo_ref, out_ref,
    own, right, left, left32, comb, gate,
    own_send, fwd_send, recv, lsend, lrecv,
):
    hid = wo_ref.shape[0]
    half = n // 2
    deep = n // 2
    span = deep // 2
    row, c = lax.axis_index("row"), lax.axis_index("col")
    z, y = row // 2, row % 2
    has_up, has_down = z < deep - 1, z > 0
    barrier = pltpu.get_barrier_semaphore()

    def greet(r, cc):
        pl.semaphore_signal(barrier, inc=1, device_id={"row": r, "col": cc}, device_id_type=MESH)

    greet(row, 1 - c)
    for cc in range(2):
        greet(2 * z + 1 - y, cc)

    @pl.when(has_up)
    def _():
        for cc in range(2):
            greet(row + 2, cc)

    @pl.when(has_down)
    def _():
        for cc in range(2):
            greet(row - 2, cc)

    normed = layer_norm(x_ref[...].astype(F32)).astype(BF16)
    proj = jnp.dot(normed, wp_ref[:, 2 * hid :], preferred_element_type=F32)
    mine = (jax.nn.sigmoid(proj[:, :hid]) * proj[:, hid:]).astype(BF16)
    own[...] = mine
    dest = z // span
    my_slot = row - dest * half

    @pl.when(dest == c)
    def _():
        right[my_slot, c] = mine

    step = rows * cols // chunks
    greeted = 3 + 2 * has_up.astype(jnp.int32) + 2 * has_down.astype(jnp.int32)
    pl.semaphore_wait(barrier, greeted)

    def own_copy(way, q, r):
        return pltpu.make_async_remote_copy(
            src_ref=own.at[pl.ds(q * step, step)],
            dst_ref=right.at[my_slot, c, pl.ds(q * step, step)],
            send_sem=own_send.at[way, q],
            recv_sem=recv.at[my_slot, c, q],
            device_id={"row": r, "col": dest},
            device_id_type=MESH,
        )

    ways = ((0, has_up, row + 2), (1, has_down, row - 2), (2, None, 2 * z + 1 - y), (3, dest != c, row))
    for q in range(chunks):
        for way, cond, r in ways:
            if cond is None:
                own_copy(way, q, r).start()
            else:
                pl.when(cond)(lambda way=way, q=q, r=r: own_copy(way, q, r).start())

    proj = jnp.dot(normed, wp_ref[:, : 2 * hid], preferred_element_type=F32)
    mine = (jax.nn.sigmoid(proj[:, :hid]) * proj[:, hid:]).astype(BF16)
    left[c] = mine
    left32[c] = mine.astype(F32)
    swap = pltpu.make_async_remote_copy(
        src_ref=left.at[c], dst_ref=left.at[c], send_sem=lsend, recv_sem=lrecv,
        device_id={"row": row, "col": 1 - c}, device_id_type=MESH,
    )
    gate[...] = jax.nn.sigmoid(jnp.dot(normed, wg_ref[...], preferred_element_type=F32))
    swap.start()

    def source(t):
        low = c * span
        inside = low + lax.rem(z - low + t + deep, span)
        return jnp.where(z < low, low + t, jnp.where(z >= low + span, low + span - 1 - t, inside))

    def block(slot, kc, q, way, r):
        part = right.at[slot, kc, pl.ds(q * step, step)]
        return pltpu.make_async_remote_copy(
            src_ref=part, dst_ref=part, send_sem=fwd_send.at[slot, kc, q, way],
            recv_sem=recv.at[slot, kc, q], device_id={"row": r, "col": c}, device_id_type=MESH,
        )

    def forwards(t, act):
        zs = source(t)
        slot = zs * 2 + y - c * half

        @pl.when(zs != z)
        def _():
            for q in range(chunks):
                for kc in range(2):
                    act(zs, slot, kc, q)

    def send_on(zs, slot, kc, q):
        block(slot, kc, q, 0, row).wait_recv()

        @pl.when((zs < z) & has_up)
        def _():
            block(slot, kc, q, 0, row + 2).start()

        @pl.when((zs > z) & has_down)
        def _():
            block(slot, kc, q, 0, row - 2).start()

        block(slot, kc, q, 1, 2 * z + 1 - y).start()

    def sent(zs, slot, kc, q):
        @pl.when(((zs < z) & has_up) | ((zs > z) & has_down))
        def _():
            block(slot, kc, q, 0, row).wait_send()

        block(slot, kc, q, 1, row).wait_send()

    def compute(slot):
        @pl.loop(0, rows // 2)
        def _(pair):
            acc = [[None, None] for _ in range(rows)]
            for kc in range(2):
                wide = right[slot, kc, pl.ds(pair * 2 * cols, 2 * cols), :].astype(F32)
                for kt in range(0, cols, 8):
                    r = [wide[j * cols + kt : j * cols + kt + 8] for j in range(2)]
                    for i in range(rows):
                        l = left32[kc, i * cols + kt : i * cols + kt + 8, :]
                        for j in range(2):
                            term = l * r[j]
                            acc[i][j] = term if acc[i][j] is None else acc[i][j] + term
            for i in range(rows):
                for j in range(2):
                    comb[pl.ds(i * cols + slot * rows + pair * 2 + j, 1), :] = jnp.sum(
                        acc[i][j], axis=0, keepdims=True
                    )

    def compute_own(t):
        zs = source(t)

        @pl.when(zs == z)
        def _():
            for q in range(chunks):
                block(zs * 2 + y - c * half, 1 - c, q, 0, row).wait_recv()

        compute(zs * 2 + y - c * half)

    def compute_other(t):
        slot = source(t) * 2 + 1 - y - c * half
        for q in range(chunks):
            for kc in range(2):
                block(slot, kc, q, 0, row).wait_recv()
        compute(slot)

    forwards(0, send_on)
    pltpu.make_async_remote_copy(
        src_ref=left.at[1 - c], dst_ref=left.at[1 - c], send_sem=lsend, recv_sem=lrecv,
        device_id={"row": row, "col": 1 - c}, device_id_type=MESH,
    ).wait_recv()
    left32[1 - c] = left[1 - c].astype(F32)
    compute_own(0)

    @pl.loop(1, span)
    def _(t):
        forwards(t, send_on)
        compute_other(t - 1)
        compute_own(t)

    compute_other(span - 1)

    tri = layer_norm(comb[...]).astype(BF16)
    update = jnp.dot(tri, wo_ref[...], preferred_element_type=F32) * gate[...]
    out_ref[...] = update.astype(BF16)

    for q in range(chunks):
        for way, cond, r in ways:
            if cond is None:
                own_copy(way, q, r).wait_send()
            else:
                pl.when(cond)(lambda way=way, q=q, r=r: own_copy(way, q, r).wait_send())
    swap.wait_send()

    @pl.loop(0, span)
    def _(t):
        forwards(t, sent)


def per_device(n, pair_rep, proj_weight, gate_weight, out_weight):
    rows, cols, channels = pair_rep.shape
    hid = out_weight.shape[0]
    flat = rows * cols
    chunks = rows // 2
    vmem = pl.BlockSpec(memory_space=pltpu.VMEM)
    dma = pltpu.SemaphoreType.DMA
    out = pl.pallas_call(
        functools.partial(kernel, n, rows, cols, chunks),
        out_shape=jax.ShapeDtypeStruct((flat, channels), BF16),
        in_specs=[vmem] * 4,
        out_specs=vmem,
        scratch_shapes=[
            pltpu.VMEM((flat, hid), BF16),
            pltpu.VMEM((n // 2, 2, flat, hid), BF16),
            pltpu.VMEM((2, flat, hid), BF16),
            pltpu.VMEM((2, flat, hid), F32),
            pltpu.VMEM((flat, hid), F32),
            pltpu.VMEM((flat, channels), F32),
            dma((4, chunks)),
            dma((n // 2, 2, chunks, 2)),
            dma((n // 2, 2, chunks)),
            dma,
            dma,
        ],
        compiler_params=pltpu.CompilerParams(
            collective_id=0, has_side_effects=True, vmem_limit_bytes=60 * 1024 * 1024
        ),
    )(pair_rep.reshape(flat, channels), proj_weight, gate_weight, out_weight)
    return out.reshape(rows, cols, channels)


def solution(mesh):
    placed = (P(("groups", "row"), "col", None), P(), P(), P())
    return jax.shard_map(
        functools.partial(per_device, mesh.shape["row"]),
        mesh=mesh,
        in_specs=placed,
        out_specs=P(("groups", "row"), "col", None),
        check_vma=False,
    )
```

time: 72.6 us -> 21.2 us (0.29)
  the two profiles are of different devices: /device:TPU:0 before, /device:TPU:1 now
where the time goes in v1:
time: 21.2 us; the launch traced here: 21 us
  Pallas kernels  19.4 us (92%)
  local copies, waits for them, and re-layouts  1.55 us (7%)
    pallas_call x1, Pallas kernels, per_device(): pl.pallas_call(functools.partial(kernel, n, rows, cols, chunks), out_shap...  19.4 us
    unnamed x1, local copies, waits for them, and re-layouts  1.55 us

profile of v1, /device:TPU:1, one launch (start us, length us, event | category | flops | bytes accessed | tf_op | source)
XLA Modules:
  0.0 21.0 jit_solution(2030979923521840601)
XLA Ops:
  0.0 19.4 %shard_map.46 = bf16[400,128]{1,0:T(8,128)(2,1)} custom-call(bf16[400,128]{1,0:T(8,128)(2,1)} %bitcast.3, bf16[128,512]{1,0:T(8,128)(2,1)} %wp_ref.1, bf16[128,128]{1,0:T(8,128)(2,1)} %wg_ref.1, bf16[128,128]{1,0:T(8,128)(2,1)} %wo_ref.1), custom_call_target="tpu_custom_call" | custom-call | tf_op jit(solution)/shard_map/pallas_call | solution.py:215
  19.5 1.5 %copy.6 = bf16[10,40,128]{2,1,0:T(8,128)(2,1)} copy(bf16[10,40,128]{2,1,0:T(8,128)(2,1)} %bitcast.2) | data formatting | bytes 204800

commit v2 on v1

v2 whole, which is shorter than its diff:
```python
import functools

import jax
import jax.numpy as jnp
from jax import lax
from jax.experimental import pallas as pl
from jax.experimental.pallas import tpu as pltpu
from jax.sharding import PartitionSpec as P

MESH = pl.DeviceIdType.MESH
F32 = jnp.float32
BF16 = jnp.bfloat16


def layer_norm(values):
    average = jnp.mean(values, axis=-1, keepdims=True)
    centered = values - average
    spread = jnp.mean(centered * centered, axis=-1, keepdims=True)
    return centered * lax.rsqrt(spread + 1e-05)


def kernel(
    n, rows, cols, chunks, x_ref, wp_ref, wg_ref, wo_ref, out_ref,
    own, right, left, left32, comb, gate, stage, back,
    own_send, fwd_send, recv, lsend, lrecv, ret_send, ret_recv,
):
    hid = wo_ref.shape[0]
    deep = n // 2
    span = deep // 2
    row, c = lax.axis_index("row"), lax.axis_index("col")
    z, y = row // 2, row % 2
    across = 2 * z + 1 - y
    has_up, has_down = z < deep - 1, z > 0
    low = c * span
    barrier = pltpu.get_barrier_semaphore()

    def greet(r, cc):
        pl.semaphore_signal(barrier, inc=1, device_id={"row": r, "col": cc}, device_id_type=MESH)

    greet(row, 1 - c)
    greet(across, c)

    @pl.when(has_up)
    def _():
        for cc in range(2):
            greet(row + 2, cc)

    @pl.when(has_down)
    def _():
        for cc in range(2):
            greet(row - 2, cc)

    normed = layer_norm(x_ref[...].astype(F32)).astype(BF16)
    proj = jnp.dot(normed, wp_ref[:, 2 * hid :], preferred_element_type=F32)
    mine = (jax.nn.sigmoid(proj[:, :hid]) * proj[:, hid:]).astype(BF16)
    own[...] = mine
    dest = z // span
    my_slot = z - dest * span

    @pl.when(dest == c)
    def _():
        right[my_slot, c] = mine

    step = rows * cols // chunks
    greeted = 2 + 2 * has_up.astype(jnp.int32) + 2 * has_down.astype(jnp.int32)
    pl.semaphore_wait(barrier, greeted)

    def own_copy(way, q, r):
        return pltpu.make_async_remote_copy(
            src_ref=own.at[pl.ds(q * step, step)],
            dst_ref=right.at[my_slot, c, pl.ds(q * step, step)],
            send_sem=own_send.at[way, q],
            recv_sem=recv.at[my_slot, c, q],
            device_id={"row": r, "col": dest},
            device_id_type=MESH,
        )

    ways = ((0, has_up, row + 2), (1, has_down, row - 2), (2, dest != c, row))
    for q in range(chunks):
        for way, cond, r in ways:
            pl.when(cond)(lambda way=way, q=q, r=r: own_copy(way, q, r).start())

    def left_copy(which, kc, way, r, cc):
        part = left.at[which, kc]
        return pltpu.make_async_remote_copy(
            src_ref=part, dst_ref=part, send_sem=lsend.at[way], recv_sem=lrecv.at[which, kc],
            device_id={"row": r, "col": cc}, device_id_type=MESH,
        )

    proj = jnp.dot(normed, wp_ref[:, : 2 * hid], preferred_element_type=F32)
    mine = (jax.nn.sigmoid(proj[:, :hid]) * proj[:, hid:]).astype(BF16)
    left[y, c] = mine
    left32[y, c] = mine.astype(F32)
    gate[...] = jax.nn.sigmoid(jnp.dot(normed, wg_ref[...], preferred_element_type=F32))
    left_copy(y, c, 0, across, c).start()
    left_copy(y, c, 1, row, 1 - c).start()

    def source(t):
        inside = low + lax.rem(z - low + t + 1 + deep, span)
        return jnp.where(z < low, low + t, jnp.where(z >= low + span, low + span - 1 - t, inside))

    def passes(zs):
        return ((zs < z) & has_up) | ((zs > z) & has_down)

    def block(slot, kc, q, r):
        part = right.at[slot, kc, pl.ds(q * step, step)]
        return pltpu.make_async_remote_copy(
            src_ref=part, dst_ref=part, send_sem=fwd_send.at[slot, kc, q],
            recv_sem=recv.at[slot, kc, q], device_id={"row": r, "col": c}, device_id_type=MESH,
        )

    def send_on(t, q):
        zs = source(t)

        @pl.when(passes(zs))
        def _():
            for kc in range(2):
                block(zs - low, kc, q, row).wait_recv()
                block(zs - low, kc, q, jnp.where(zs < z, row + 2, row - 2)).start()

    early = chunks - 2
    for q in range(early):
        send_on(0, q)
    left_copy(1 - y, c, 2, row, 1 - c).wait_recv()
    left_copy(1 - y, c, 2, row, 1 - c).start()
    for q in range(early, chunks):
        send_on(0, q)

    @pl.loop(1, span)
    def _(t):
        for q in range(chunks):
            send_on(t, q)

    left32[1 - y, c] = left[1 - y, c].astype(F32)
    for which in (y, 1 - y):
        left_copy(which, 1 - c, 0, row, c).wait_recv()
        left32[which, 1 - c] = left[which, 1 - c].astype(F32)

    def ret_copy(slot, pair):
        return pltpu.make_async_remote_copy(
            src_ref=stage.at[slot, pair], dst_ref=back.at[slot, pair],
            send_sem=ret_send.at[slot, pair], recv_sem=ret_recv.at[slot, pair],
            device_id={"row": across, "col": c}, device_id_type=MESH,
        )

    def sums(which, slot, pair, put):
        acc = [[None, None] for _ in range(rows)]
        for kc in range(2):
            wide = right[slot, kc, pl.ds(pair * 2 * cols, 2 * cols), :].astype(F32)
            for kt in range(0, cols, 8):
                r = [wide[j * cols + kt : j * cols + kt + 8] for j in range(2)]
                for i in range(rows):
                    l = left32[which, kc, i * cols + kt : i * cols + kt + 8, :]
                    for j in range(2):
                        term = l * r[j]
                        acc[i][j] = term if acc[i][j] is None else acc[i][j] + term
        for i in range(rows):
            for j in range(2):
                put(i, j, jnp.sum(acc[i][j], axis=0, keepdims=True))

    def place(i, j, slot, pair, side, value):
        comb[pl.ds(i * cols + (slot * 2 + side) * rows + pair * 2 + j, 1), :] = value

    @pl.loop(0, span)
    def _(t):
        zs = source(lax.rem(t + jnp.where((z >= low) & (z < low + span), span - 1, 0), span))
        slot = zs - low

        @pl.loop(0, chunks)
        def _(pair):
            for kc in range(2):
                @pl.when(jnp.logical_not(passes(zs)) & ((zs != z) | (c != kc)))
                def _(kc=kc):
                    block(slot, kc, pair, row).wait_recv()

            def put_stage(i, j, value):
                stage[slot, pair, j * rows + i : j * rows + i + 1, :] = value

            sums(1 - y, slot, pair, put_stage)
            sums(y, slot, pair, lambda i, j, value: place(i, j, slot, pair, y, value))
            ret_copy(slot, pair).start()

    @pl.loop(0, span)
    def _(t):
        slot = source(lax.rem(t + jnp.where((z >= low) & (z < low + span), span - 1, 0), span)) - low

        @pl.loop(0, chunks)
        def _(pair):
            ret_copy(slot, pair).wait_recv()
            for i in range(rows):
                for j in range(2):
                    got = back[slot, pair, j * rows + i : j * rows + i + 1, :]
                    place(i, j, slot, pair, 1 - y, got)

    tri = layer_norm(comb[...]).astype(BF16)
    update = jnp.dot(tri, wo_ref[...], preferred_element_type=F32) * gate[...]
    out_ref[...] = update.astype(BF16)

    for q in range(chunks):
        for way, cond, r in ways:
            pl.when(cond)(lambda way=way, q=q, r=r: own_copy(way, q, r).wait_send())
    left_copy(y, c, 0, across, c).wait_send()
    left_copy(y, c, 1, row, 1 - c).wait_send()
    left_copy(1 - y, c, 2, row, 1 - c).wait_send()

    @pl.loop(0, span)
    def _(slot):
        @pl.when(passes(slot + low))
        def _():
            for q in range(chunks):
                for kc in range(2):
                    block(slot, kc, q, row).wait_send()

        for q in range(chunks):
            ret_copy(slot, q).wait_send()


def per_device(n, pair_rep, proj_weight, gate_weight, out_weight):
    rows, cols, channels = pair_rep.shape
    hid = out_weight.shape[0]
    flat = rows * cols
    chunks = rows // 2
    span = n // 4
    padded = -(-2 * rows // 8) * 8
    vmem = pl.BlockSpec(memory_space=pltpu.VMEM)
    dma = pltpu.SemaphoreType.DMA
    out = pl.pallas_call(
        functools.partial(kernel, n, rows, cols, chunks),
        out_shape=jax.ShapeDtypeStruct((flat, channels), BF16),
        in_specs=[vmem] * 4,
        out_specs=vmem,
        scratch_shapes=[
            pltpu.VMEM((flat, hid), BF16),
            pltpu.VMEM((span, 2, flat, hid), BF16),
            pltpu.VMEM((2, 2, flat, hid), BF16),
            pltpu.VMEM((2, 2, flat, hid), F32),
            pltpu.VMEM((flat, hid), F32),
            pltpu.VMEM((flat, channels), F32),
            pltpu.VMEM((span, chunks, padded, hid), F32),
            pltpu.VMEM((span, chunks, padded, hid), F32),
            dma((3, chunks)),
            dma((span, 2, chunks)),
            dma((span, 2, chunks)),
            dma((3,)),
            dma((2, 2)),
            dma((span, chunks)),
            dma((span, chunks)),
        ],
        compiler_params=pltpu.CompilerParams(
            collective_id=0, has_side_effects=True, vmem_limit_bytes=60 * 1024 * 1024
        ),
    )(pair_rep.reshape(flat, channels), proj_weight, gate_weight, out_weight)
    return out.reshape(rows, cols, channels)


def solution(mesh):
    placed = (P(("groups", "row"), "col", None), P(), P(), P())
    return jax.shard_map(
        functools.partial(per_device, mesh.shape["row"]),
        mesh=mesh,
        in_specs=placed,
        out_specs=P(("groups", "row"), "col", None),
        check_vma=False,
    )
```

time: 21.2 us -> 19.9 us (0.939)
  Pallas kernels: 19.4 us -> 18.2 us
    pallas_call x1, Pallas kernels: 19.4 us -> 18.2 us  [per_device(): pl.pallas_call(functools.partial(kernel, n, rows, cols, chunks), out_shap...]
where the time goes in v2:
time: 19.9 us; the launch traced here: 19.8 us
  Pallas kernels  18.2 us (91%)
  local copies, waits for them, and re-layouts  1.55 us (8%)
    pallas_call x1, Pallas kernels, per_device(): pl.pallas_call(functools.partial(kernel, n, rows, cols, chunks), out_shap...  18.2 us
    unnamed x1, local copies, waits for them, and re-layouts  1.55 us

profile of v2, /device:TPU:1, one launch (start us, length us, event | category | flops | bytes accessed | tf_op | source)
XLA Modules:
  0.0 19.8 jit_solution(1950046437699303)
XLA Ops:
  0.0 18.2 %shard_map.46 = bf16[400,128]{1,0:T(8,128)(2,1)} custom-call(bf16[400,128]{1,0:T(8,128)(2,1)} %bitcast.3, bf16[128,512]{1,0:T(8,128)(2,1)} %wp_ref.1, bf16[128,128]{1,0:T(8,128)(2,1)} %wg_ref.1, bf16[128,128]{1,0:T(8,128)(2,1)} %wo_ref.1), custom_call_target="tpu_custom_call" | custom-call | tf_op jit(solution)/shard_map/pallas_call | solution.py:227
  18.2 1.5 %copy.6 = bf16[10,40,128]{2,1,0:T(8,128)(2,1)} copy(bf16[10,40,128]{2,1,0:T(8,128)(2,1)} %bitcast.2) | data formatting | bytes 204800

commit v3 on v2

--- a/solution.py
+++ b/solution.py
@@ -20,11 +20,22 @@
 
 
 def kernel(
-    n, rows, cols, chunks, x_ref, wp_ref, wg_ref, wo_ref, out_ref,
-    own, right, left, left32, comb, gate, stage, back,
+    n, rows, cols, pairs, sub, x_hbm, wp_hbm, wg_hbm, wo_hbm, out_ref,
+    x_ref, wp_ref, wg_ref, wo_ref, normed, in_sem, own, right, left, left32, comb, gate, stage, back,
     own_send, fwd_send, recv, lsend, lrecv, ret_send, ret_recv,
 ):
     hid = wo_ref.shape[0]
+    chunks = pairs * sub
+    flat = rows * cols
+    part = flat // pairs
+    loads = [pltpu.make_async_copy(x_hbm, x_ref, in_sem.at[0])]
+    for k in (1, 0):
+        cut = (slice(None), pl.ds(2 * hid * k, 2 * hid))
+        loads.append(pltpu.make_async_copy(wp_hbm.at[cut], wp_ref.at[k], in_sem.at[len(loads)]))
+    loads.append(pltpu.make_async_copy(wg_hbm, wg_ref, in_sem.at[3]))
+    loads.append(pltpu.make_async_copy(wo_hbm, wo_ref, in_sem.at[4]))
+    for load in loads:
+        load.start()
     deep = n // 2
     span = deep // 2
     row, c = lax.axis_index("row"), lax.axis_index("col")
@@ -50,20 +61,22 @@
         for cc in range(2):
             greet(row - 2, cc)
 
-    normed = layer_norm(x_ref[...].astype(F32)).astype(BF16)
-    proj = jnp.dot(normed, wp_ref[:, 2 * hid :], preferred_element_type=F32)
-    mine = (jax.nn.sigmoid(proj[:, :hid]) * proj[:, hid:]).astype(BF16)
-    own[...] = mine
     dest = z // span
     my_slot = z - dest * span
-
-    @pl.when(dest == c)
-    def _():
-        right[my_slot, c] = mine
-
-    step = rows * cols // chunks
-    greeted = 2 + 2 * has_up.astype(jnp.int32) + 2 * has_down.astype(jnp.int32)
-    pl.semaphore_wait(barrier, greeted)
+    step = flat // chunks
+
+    def gated(values, k):
+        proj = jnp.dot(values, wp_ref[k], preferred_element_type=F32)
+        return (jax.nn.sigmoid(proj[:, :hid]) * proj[:, hid:]).astype(BF16)
+
+    def prepare(p):
+        here = pl.ds(p * part, part)
+        values = layer_norm(x_ref[here, :].astype(F32)).astype(BF16)
+        normed[here, :] = values
+        own[here, :] = gated(values, 1)
+
+    loads[0].wait()
+    loads[1].wait()
 
     def own_copy(way, q, r):
         return pltpu.make_async_remote_copy(
@@ -75,10 +88,26 @@
             device_id_type=MESH,
         )
 
-    ways = ((0, has_up, row + 2), (1, has_down, row - 2), (2, dest != c, row))
-    for q in range(chunks):
+    ways = ((0, has_down, row - 2), (1, has_up, row + 2), (2, dest != c, row))
+
+    def own_all(p, act):
         for way, cond, r in ways:
-            pl.when(cond)(lambda way=way, q=q, r=r: own_copy(way, q, r).start())
+            @pl.when(cond)
+            def _(way=way, r=r):
+                for q in range(p * sub, (p + 1) * sub):
+                    act(own_copy(way, q, r))
+
+    prepare(0)
+    greeted = 2 + 2 * has_up.astype(jnp.int32) + 2 * has_down.astype(jnp.int32)
+    pl.semaphore_wait(barrier, greeted)
+    for p in range(1, pairs):
+        prepare(p)
+        own_all(p - 1, lambda copy: copy.start())
+    own_all(pairs - 1, lambda copy: copy.start())
+
+    @pl.when(dest == c)
+    def _():
+        right[my_slot, c] = own[...]
 
     def left_copy(which, kc, way, r, cc):
         part = left.at[which, kc]
@@ -87,11 +116,12 @@
             device_id={"row": r, "col": cc}, device_id_type=MESH,
         )
 
-    proj = jnp.dot(normed, wp_ref[:, : 2 * hid], preferred_element_type=F32)
-    mine = (jax.nn.sigmoid(proj[:, :hid]) * proj[:, hid:]).astype(BF16)
+    loads[2].wait()
+    loads[3].wait()
+    mine = gated(normed[...], 0)
     left[y, c] = mine
     left32[y, c] = mine.astype(F32)
-    gate[...] = jax.nn.sigmoid(jnp.dot(normed, wg_ref[...], preferred_element_type=F32))
+    gate[...] = jax.nn.sigmoid(jnp.dot(normed[...], wg_ref[...], preferred_element_type=F32))
     left_copy(y, c, 0, across, c).start()
     left_copy(y, c, 1, row, 1 - c).start()
 
@@ -118,18 +148,15 @@
                 block(zs - low, kc, q, row).wait_recv()
                 block(zs - low, kc, q, jnp.where(zs < z, row + 2, row - 2)).start()
 
-    early = chunks - 2
-    for q in range(early):
-        send_on(0, q)
+    early = chunks - 2 * sub
+    pl.loop(0, early)(lambda q: send_on(0, q))
     left_copy(1 - y, c, 2, row, 1 - c).wait_recv()
     left_copy(1 - y, c, 2, row, 1 - c).start()
-    for q in range(early, chunks):
-        send_on(0, q)
+    pl.loop(early, chunks)(lambda q: send_on(0, q))
 
     @pl.loop(1, span)
     def _(t):
-        for q in range(chunks):
-            send_on(t, q)
+        pl.loop(0, chunks)(lambda q: send_on(t, q))
 
     left32[1 - y, c] = left[1 - y, c].astype(F32)
     for which in (y, 1 - y):
@@ -166,12 +193,13 @@
         zs = source(lax.rem(t + jnp.where((z >= low) & (z < low + span), span - 1, 0), span))
         slot = zs - low
 
-        @pl.loop(0, chunks)
+        @pl.loop(0, pairs)
         def _(pair):
             for kc in range(2):
                 @pl.when(jnp.logical_not(passes(zs)) & ((zs != z) | (c != kc)))
                 def _(kc=kc):
-                    block(slot, kc, pair, row).wait_recv()
+                    for q in range(sub):
+                        block(slot, kc, pair * sub + q, row).wait_recv()
 
             def put_stage(i, j, value):
                 stage[slot, pair, j * rows + i : j * rows + i + 1, :] = value
@@ -184,7 +212,7 @@
     def _(t):
         slot = source(lax.rem(t + jnp.where((z >= low) & (z < low + span), span - 1, 0), span)) - low
 
-        @pl.loop(0, chunks)
+        @pl.loop(0, pairs)
         def _(pair):
             ret_copy(slot, pair).wait_recv()
             for i in range(rows):
@@ -192,13 +220,13 @@
                     got = back[slot, pair, j * rows + i : j * rows + i + 1, :]
                     place(i, j, slot, pair, 1 - y, got)
 
+    loads[4].wait()
     tri = layer_norm(comb[...]).astype(BF16)
     update = jnp.dot(tri, wo_ref[...], preferred_element_type=F32) * gate[...]
     out_ref[...] = update.astype(BF16)
 
-    for q in range(chunks):
-        for way, cond, r in ways:
-            pl.when(cond)(lambda way=way, q=q, r=r: own_copy(way, q, r).wait_send())
+    for p in range(pairs):
+        own_all(p, lambda copy: copy.wait_send())
     left_copy(y, c, 0, across, c).wait_send()
     left_copy(y, c, 1, row, 1 - c).wait_send()
     left_copy(1 - y, c, 2, row, 1 - c).wait_send()
@@ -207,44 +235,53 @@
     def _(slot):
         @pl.when(passes(slot + low))
         def _():
-            for q in range(chunks):
+            @pl.loop(0, chunks)
+            def _(q):
                 for kc in range(2):
                     block(slot, kc, q, row).wait_send()
 
-        for q in range(chunks):
-            ret_copy(slot, q).wait_send()
+        for pair in range(pairs):
+            ret_copy(slot, pair).wait_send()
 
 
 def per_device(n, pair_rep, proj_weight, gate_weight, out_weight):
     rows, cols, channels = pair_rep.shape
     hid = out_weight.shape[0]
     flat = rows * cols
-    chunks = rows // 2
+    pairs = rows // 2
+    sub = 1
+    chunks = pairs * sub
     span = n // 4
     padded = -(-2 * rows // 8) * 8
     vmem = pl.BlockSpec(memory_space=pltpu.VMEM)
     dma = pltpu.SemaphoreType.DMA
     out = pl.pallas_call(
-        functools.partial(kernel, n, rows, cols, chunks),
-        out_shape=jax.ShapeDtypeStruct((flat, channels), BF16),
-        in_specs=[vmem] * 4,
+        functools.partial(kernel, n, rows, cols, pairs, sub),
+        out_shape=pltpu.VMEM((flat, channels), BF16),
+        in_specs=[pl.BlockSpec(memory_space=pl.ANY)] * 4,
         out_specs=vmem,
         scratch_shapes=[
+            pltpu.VMEM((flat, channels), BF16),
+            pltpu.VMEM((2, channels, 2 * hid), BF16),
+            pltpu.VMEM((channels, channels), BF16),
+            pltpu.VMEM((hid, channels), BF16),
+            pltpu.VMEM((flat, channels), BF16),
+            dma((5,)),
             pltpu.VMEM((flat, hid), BF16),
             pltpu.VMEM((span, 2, flat, hid), BF16),
             pltpu.VMEM((2, 2, flat, hid), BF16),
             pltpu.VMEM((2, 2, flat, hid), F32),
             pltpu.VMEM((flat, hid), F32),
             pltpu.VMEM((flat, channels), F32),
-            pltpu.VMEM((span, chunks, padded, hid), F32),
-            pltpu.VMEM((span, chunks, padded, hid), F32),
+            pltpu.VMEM((span, pairs, padded, hid), F32),
+            pltpu.VMEM((span, pairs, padded, hid), F32),
             dma((3, chunks)),
             dma((span, 2, chunks)),
             dma((span, 2, chunks)),
             dma((3,)),
             dma((2, 2)),
-            dma((span, chunks)),
-            dma((span, chunks)),
+            dma((span, pairs)),
+            dma((span, pairs)),
         ],
         compiler_params=pltpu.CompilerParams(
             collective_id=0, has_side_effects=True, vmem_limit_bytes=60 * 1024 * 1024

time: 19.9 us -> 17.9 us (0.90)
  Pallas kernels: 18.2 us -> 17.1 us
  local copies, waits for them, and re-layouts: 1.55 us -> 0.64 us
    pallas_call x1, Pallas kernels: 18.2 us -> 17.1 us  [per_device(): pl.pallas_call(functools.partial(kernel, n, rows, cols, pairs, sub), out_...]
    unnamed x1, local copies, waits for them, and re-layouts: 1.55 us -> 0.64 us
where the time goes in v3:
time: 17.9 us; the launch traced here: 17.8 us
  Pallas kernels  17.1 us (96%)
  local copies, waits for them, and re-layouts  0.64 us (4%)
    pallas_call x1, Pallas kernels, per_device(): pl.pallas_call(functools.partial(kernel, n, rows, cols, pairs, sub), out_...  17.1 us
    unnamed x1, local copies, waits for them, and re-layouts  0.64 us

profile of v3, /device:TPU:1, one launch (start us, length us, event | category | flops | bytes accessed | tf_op | source)
XLA Modules:
  0.0 17.8 jit_solution(6772698709418597086)
XLA Ops:
  0.0 17.1 %shard_map.46 = bf16[400,128]{1,0:T(8,128)(2,1)S(1)} custom-call(bf16[400,128]{1,0:T(8,128)(2,1)} %bitcast.3, bf16[128,512]{1,0:T(8,128)(2,1)} %wp_hbm.1, bf16[128,128]{1,0:T(8,128)(2,1)} %wg_hbm.1, bf16[128,128]{1,0:T(8,128)(2,1)} %wo_hbm.1), custom_call_target="tpu_custom_call" | custom-call | tf_op jit(solution)/shard_map/pallas_call | solution.py:258
  17.2 0.6 %copy.6 = bf16[10,40,128]{2,1,0:T(8,128)(2,1)} copy(bf16[10,40,128]{2,1,0:T(8,128)(2,1)S(1)} %bitcast.2) | data formatting | bytes 204800

commit v4 on v3

--- a/solution.py
+++ b/solution.py
@@ -21,20 +21,24 @@
 
 def kernel(
     n, rows, cols, pairs, sub, x_hbm, wp_hbm, wg_hbm, wo_hbm, out_ref,
-    x_ref, wp_ref, wg_ref, wo_ref, normed, in_sem, own, right, left, left32, comb, gate, stage, back,
+    x_ref, wp_ref, wg_ref, wo_ref, normed, in_sem, x_sem, own, right, left, left32, comb, gate, stage, back,
     own_send, fwd_send, recv, lsend, lrecv, ret_send, ret_recv,
 ):
     hid = wo_ref.shape[0]
     chunks = pairs * sub
     flat = rows * cols
     part = flat // pairs
-    loads = [pltpu.make_async_copy(x_hbm, x_ref, in_sem.at[0])]
+    x_loads = [
+        pltpu.make_async_copy(x_hbm.at[pl.ds(p * part, part)], x_ref.at[pl.ds(p * part, part)], x_sem.at[p])
+        for p in range(pairs)
+    ]
+    loads = []
     for k in (1, 0):
         cut = (slice(None), pl.ds(2 * hid * k, 2 * hid))
         loads.append(pltpu.make_async_copy(wp_hbm.at[cut], wp_ref.at[k], in_sem.at[len(loads)]))
-    loads.append(pltpu.make_async_copy(wg_hbm, wg_ref, in_sem.at[3]))
-    loads.append(pltpu.make_async_copy(wo_hbm, wo_ref, in_sem.at[4]))
-    for load in loads:
+    loads.append(pltpu.make_async_copy(wg_hbm, wg_ref, in_sem.at[2]))
+    loads.append(pltpu.make_async_copy(wo_hbm, wo_ref, in_sem.at[3]))
+    for load in [x_loads[0], loads[0]] + x_loads[1:] + loads[1:]:
         load.start()
     deep = n // 2
     span = deep // 2
@@ -70,13 +74,13 @@
         return (jax.nn.sigmoid(proj[:, :hid]) * proj[:, hid:]).astype(BF16)
 
     def prepare(p):
+        x_loads[p].wait()
         here = pl.ds(p * part, part)
         values = layer_norm(x_ref[here, :].astype(F32)).astype(BF16)
         normed[here, :] = values
         own[here, :] = gated(values, 1)
 
     loads[0].wait()
-    loads[1].wait()
 
     def own_copy(way, q, r):
         return pltpu.make_async_remote_copy(
@@ -100,9 +104,11 @@
     prepare(0)
     greeted = 2 + 2 * has_up.astype(jnp.int32) + 2 * has_down.astype(jnp.int32)
     pl.semaphore_wait(barrier, greeted)
+    own_all(0, lambda copy: copy.start())
     for p in range(1, pairs):
         prepare(p)
-        own_all(p - 1, lambda copy: copy.start())
+        if p > 1:
+            own_all(p - 1, lambda copy: copy.start())
     own_all(pairs - 1, lambda copy: copy.start())
 
     @pl.when(dest == c)
@@ -116,12 +122,11 @@
             device_id={"row": r, "col": cc}, device_id_type=MESH,
         )
 
+    loads[1].wait()
     loads[2].wait()
-    loads[3].wait()
     mine = gated(normed[...], 0)
     left[y, c] = mine
     left32[y, c] = mine.astype(F32)
-    gate[...] = jax.nn.sigmoid(jnp.dot(normed[...], wg_ref[...], preferred_element_type=F32))
     left_copy(y, c, 0, across, c).start()
     left_copy(y, c, 1, row, 1 - c).start()
 
@@ -148,7 +153,7 @@
                 block(zs - low, kc, q, row).wait_recv()
                 block(zs - low, kc, q, jnp.where(zs < z, row + 2, row - 2)).start()
 
-    early = chunks - 2 * sub
+    early = chunks - sub
     pl.loop(0, early)(lambda q: send_on(0, q))
     left_copy(1 - y, c, 2, row, 1 - c).wait_recv()
     left_copy(1 - y, c, 2, row, 1 - c).start()
@@ -158,6 +163,7 @@
     def _(t):
         pl.loop(0, chunks)(lambda q: send_on(t, q))
 
+    gate[...] = jax.nn.sigmoid(jnp.dot(normed[...], wg_ref[...], preferred_element_type=F32))
     left32[1 - y, c] = left[1 - y, c].astype(F32)
     for which in (y, 1 - y):
         left_copy(which, 1 - c, 0, row, c).wait_recv()
@@ -220,7 +226,7 @@
                     got = back[slot, pair, j * rows + i : j * rows + i + 1, :]
                     place(i, j, slot, pair, 1 - y, got)
 
-    loads[4].wait()
+    loads[3].wait()
     tri = layer_norm(comb[...]).astype(BF16)
     update = jnp.dot(tri, wo_ref[...], preferred_element_type=F32) * gate[...]
     out_ref[...] = update.astype(BF16)
@@ -266,7 +272,8 @@
             pltpu.VMEM((channels, channels), BF16),
             pltpu.VMEM((hid, channels), BF16),
             pltpu.VMEM((flat, channels), BF16),
-            dma((5,)),
+            dma((4,)),
+            dma((pairs,)),
             pltpu.VMEM((flat, hid), BF16),
             pltpu.VMEM((span, 2, flat, hid), BF16),
             pltpu.VMEM((2, 2, flat, hid), BF16),

time: 17.9 us -> 18 us (level)
  no operation moved by 1% of the time
where the time goes in v4:
time: 18 us; the launch traced here: 17.8 us
  Pallas kernels  17.2 us (96%)
  local copies, waits for them, and re-layouts  0.64 us (4%)
    pallas_call x1, Pallas kernels, per_device(): pl.pallas_call(functools.partial(kernel, n, rows, cols, pairs, sub), out_...  17.2 us
    unnamed x1, local copies, waits for them, and re-layouts  0.64 us

profile of v4, /device:TPU:1, one launch (start us, length us, event | category | flops | bytes accessed | tf_op | source)
XLA Modules:
  0.0 17.8 jit_solution(14451802623545735896)
XLA Ops:
  0.0 17.2 %shard_map.46 = bf16[400,128]{1,0:T(8,128)(2,1)S(1)} custom-call(bf16[400,128]{1,0:T(8,128)(2,1)} %bitcast.3, bf16[128,512]{1,0:T(8,128)(2,1)} %wp_hbm.1, bf16[128,128]{1,0:T(8,128)(2,1)} %wg_hbm.1, bf16[128,128]{1,0:T(8,128)(2,1)} %wo_hbm.1), custom_call_target="tpu_custom_call" | custom-call | tf_op jit(solution)/shard_map/pallas_call | solution.py:264
  17.2 0.6 %copy.6 = bf16[10,40,128]{2,1,0:T(8,128)(2,1)} copy(bf16[10,40,128]{2,1,0:T(8,128)(2,1)S(1)} %bitcast.2) | data formatting | bytes 204800
